TPU v7x, 512 devices: a whole 4x4x16 slice. The times are simulated.
512 devices in a mesh: replica: 64 (over z_hi, y, x, core), tensor: 8 (over z_lo).
Axes of the slice: x: 4, y: 4, z: 16 (z_hi: 2, z_lo: 8; z = z_hi * 8 + z_lo), core: 2. Of those that a mesh axis runs over, the one named last changes fastest.
Arguments:
- tokens: bfloat16 [32768, 8192], P(('replica', 'tensor')), may hold values from -6 to 6
- norm_gain: bfloat16 [8192], replicated, may hold values from 0.099609375 to 1.8984375
- key_weight: bfloat16 [64, 8192, 1024], P('replica', None, 'tensor'), may hold values from -0.0625 to 0.0625
- inner_params: bfloat16 [64, 8, 1024, 512], P('replica', 'tensor'), may hold values from -16 to 16
- outer_params: float32 [8, 1024, 512], P('tensor', 'replica'), may hold values from -6 to 6
- outer_momentum: float32 [8, 1024, 512], P('tensor', 'replica'), may hold values from -3 to 3
Outputs:
- key_rows: bfloat16 [32768, 1024], P('replica', 'tensor')
- new_outer: float32 [8, 1024, 512], P('tensor', 'replica')
- new_momentum: float32 [8, 1024, 512], P('tensor', 'replica')
- synced_params: bfloat16 [8, 1024, 512], P('tensor')
All inputs are finite; a program needn't handle non-finite values.
Results may differ from a plain program's by a relative error of at most 0.0049.
Values may be sent and summed in bfloat16 or wider, within the bound.
No kernel may reach another device: no remote copies, remote signals or barrier semaphores. Data moves between devices by JAX's collectives and lax.ppermute only.
A program may use at most 64 MiB of HBM per device.

v0:
```python
import math
import jax
import jax.numpy as jnp
from jax import lax
from jax.sharding import PartitionSpec as P

HD = 128
EPSILON = 1e-05
ROPE_BASE = 500000.0
LR_OUTER = 0.7
MOMENTUM_OUTER = 0.9


def rotate(keys_f32, positions):
    rows = keys_f32.shape[0]
    cols = keys_f32.shape[1]
    half = HD // 2
    shaped = keys_f32.reshape(rows, cols // HD, HD)
    index = jnp.arange(half).astype(jnp.float32)
    inverse = jnp.exp(-(2.0 * index / HD) * math.log(ROPE_BASE))
    angles = positions[:, None] * inverse[None, :]
    cosine = jnp.cos(angles)[:, None, :]
    sine = jnp.sin(angles)[:, None, :]
    first = shaped[:, :, :half]
    second = shaped[:, :, half:]
    joined = jnp.concatenate(
        [first * cosine - second * sine, second * cosine + first * sine], axis=-1
    )
    return joined.reshape(rows, cols)


def forward_keys(tokens, norm_gain, key_weight):
    block_f32 = tokens.astype(jnp.float32)
    scale = lax.rsqrt(jnp.mean(block_f32 * block_f32, axis=-1, keepdims=True) + EPSILON)
    normed = (block_f32 * scale * norm_gain.astype(jnp.float32)).astype(jnp.bfloat16)
    weight = key_weight[0]
    piece = lax.all_gather(normed, "tensor", axis=0, tiled=True)
    projected = jnp.dot(piece, weight, preferred_element_type=jnp.float32)
    positions = jnp.arange(piece.shape[0], dtype=jnp.int32).astype(jnp.float32)
    return rotate(projected, positions).astype(jnp.bfloat16)


def nesterov(outer_rows, moment_rows, summed, replicas):
    delta = outer_rows - summed / replicas
    moment_next = MOMENTUM_OUTER * moment_rows + delta
    outer_next = outer_rows - LR_OUTER * (delta + MOMENTUM_OUTER * moment_next)
    return (outer_next, moment_next)


def owned_sum(local_params):
    return lax.psum_scatter(
        local_params.astype(jnp.float32), "replica", scatter_dimension=0, tiled=True
    )


def sync_fragment(inner_params, outer_params, outer_momentum):
    replicas = lax.axis_size("replica")
    local_params = inner_params[0, 0]
    summed = owned_sum(local_params)
    outer_next, moment_next = nesterov(outer_params[0], outer_momentum[0], summed, replicas)
    synced = lax.all_gather(outer_next.astype(jnp.bfloat16), "replica", axis=0, tiled=True)
    return (outer_next[None], moment_next[None], synced[None])


def body(tokens, norm_gain, key_weight, inner_params, outer_params, outer_momentum):
    key_rows = forward_keys(tokens, norm_gain, key_weight)
    new_outer, new_momentum, synced_params = sync_fragment(
        inner_params, outer_params, outer_momentum
    )
    return (key_rows, new_outer, new_momentum, synced_params)


def solution(mesh):
    in_specs = (
        P(("replica", "tensor"), None),
        P(),
        P("replica", None, "tensor"),
        P("replica", "tensor", None, None),
        P("tensor", "replica", None),
        P("tensor", "replica", None),
    )
    out_specs = (
        P("replica", "tensor"),
        P("tensor", "replica", None),
        P("tensor", "replica", None),
        P("tensor", None, None),
    )
    return jax.shard_map(body, mesh=mesh, in_specs=in_specs, out_specs=out_specs, check_vma=False)
```

profile of v0, /device:TPU:1, one launch (start us, length us, event | category | flops | bytes accessed | tf_op | source)
XLA Modules:
  0.0 875.6 jit_solution(4072510112862424039)
XLA Ops:
  7.2 0.0 copy-start
  7.2 0.0 copy-start.5
  7.2 0.0 copy-start.1
  7.2 0.0 reduce-scatter.2.cloned.1.call-start
  7.2 3.0 bitcast_convert_fusion
  10.2 0.0 reduce-scatter.2.cloned.1.call-update
  10.3 0.0 all-gather.5.cloned.1.call-start
  10.3 0.0 copy-done.5
  10.4 0.3 fusion
  10.7 565.8 %reduce-scatter.2.cloned.1.call-done = f32[16,512]{1,0:T(8,128)} async-done(((f32[1024,512]{1,0:T(8,128)}), f32[16,512]{1,0:T(8,128)}) %reduce-scatter.2.cloned.1.call-update) | async-done | bytes 32784 | tf_op jit(solution)/shard_map/reduce_scatter | solution.py:51
  576.5 0.0 copy-done.3
  576.5 1.4 fusion.17
  577.9 0.0 all-gather.5.cloned.1.call-update
  577.9 0.0 all-gather.3.cloned.1.call-start
  578.0 1.3 fusion.2
  579.2 0.0 all-gather.3.cloned.1.call-update
  579.3 108.2 %all-gather.5.cloned.1.call-done = bf16[1024,512]{1,0:T(8,128)(2,1)} async-done(((bf16[16,512]{1,0:T(8,128)(2,1)}), bf16[1024,512]{1,0:T(8,128)(2,1)}) %all-gather.5.cloned.1.call-update) | async-done | bytes 1048592 | tf_op jit(solution)/shard_map/all_gather | solution.py:61
  687.5 173.0 %all-gather.3.cloned.1.call-done = bf16[512,8192]{1,0:T(8,128)(2,1)} async-done(((bf16[64,8192]{1,0:T(8,128)(2,1)}), bf16[512,8192]{1,0:T(8,128)(2,1)}) %all-gather.3.cloned.1.call-update) | async-done | bytes 8388624 | tf_op jit(solution)/shard_map/all_gather | solution.py:37
  860.5 0.0 copy-done
  860.5 6.3 fusion.5
  866.8 0.6 fusion.13
  867.4 0.8 copy.10
  868.1 0.0 copy-done.2
  868.2 1.0 copy.12
  (10 shorter events, 0.0 us)
Async XLA Ops:
  7.2 853.4 %copy-start = (bf16[1,8192,128]{2,1,0:T(8,128)(2,1)S(1)}, bf16[1,8192,128]{2,1,0:T(8,128)(2,1)}, u32[]{:S(2)}) copy-start(bf16[1,8192,128]{2,1,0:T(8,128)(2,1)} %param.8) | copy-start | bytes 6291460
  7.2 3.1 copy-start.5
  7.2 3.2 copy-start.1
  7.2 569.3 %reduce-scatter.2.cloned.1.call-start = ((), (), s32[]{:S(2)}) async-start(), calls=%async_computation.2 | async-start | bytes 2129920 | tf_op jit(solution)/shard_map/reduce_scatter | solution.py:51
  10.2 566.2 %copy-start.3 = (f32[1,16,512]{2,1,0:T(8,128)S(1)}, f32[1,16,512]{2,1,0:T(8,128)}, u32[]{:S(2)}) copy-start(f32[1,16,512]{2,1,0:T(8,128)} %param.11) | copy-start | bytes 98308
  10.2 566.2 %copy-start.4 = (f32[1,16,512]{2,1,0:T(8,128)S(1)}, f32[1,16,512]{2,1,0:T(8,128)}, u32[]{:S(2)}) copy-start(f32[1,16,512]{2,1,0:T(8,128)} %param.10) | copy-start | bytes 98308
  10.3 677.2 %all-gather.5.cloned.1.call-start = ((), (), s32[]{:S(2)}) async-start(), calls=%async_computation.3 | async-start | bytes 1064960 | tf_op jit(solution)/shard_map/all_gather | solution.py:61
  577.9 282.6 %all-gather.3.cloned.1.call-start = ((), (), s32[]{:S(2)}) async-start(), calls=%async_computation.1 | async-start | bytes 9437184 | tf_op jit(solution)/shard_map/all_gather | solution.py:37
  687.5 180.6 %copy-start.2 = (bf16[1024,512]{1,0:T(8,128)(2,1)S(1)}, bf16[1024,512]{1,0:T(8,128)(2,1)}, u32[]{:S(2)}) copy-start(bf16[1024,512]{1,0:T(8,128)(2,1)} %all-gather.5.cloned.1.call-done) | copy-start | bytes 3145732
Sparse Core Ops, SparseCore 0:
  10.8 565.6 reduce-scatter.1
  582.3 105.1 all-gather.4
  690.4 170.1 all-gather.2
where the time goes:
time: 876 us
  waiting for transfers between devices  847 us (97%)
  between operations  13.8 us (2%)
    reduce_scatter x1, waiting for transfers between devices, owned_sum(): lax.psum_scatter(local_params.astype(jnp.float32), 'replica', scatter_dim...  566 us
    all_gather x1, waiting for transfers between devices, forward_keys(): piece = lax.all_gather(normed, 'tensor', axis=0, tiled=True)  173 us
    all_gather x1, waiting for transfers between devices, sync_fragment(): lax.all_gather(outer_next.astype(jnp.bfloat16), 'replica', axis=0, tiled=...  108 us
  transfers between devices with their start and end apart: 3, of which 3 were waited for; matrix products, arithmetic and copies ran while one was open for 0% of the time, Pallas kernels for 0%

commit v1 on v0

--- a/solution.py
+++ b/solution.py
@@ -58,7 +58,13 @@
     local_params = inner_params[0, 0]
     summed = owned_sum(local_params)
     outer_next, moment_next = nesterov(outer_params[0], outer_momentum[0], summed, replicas)
-    synced = lax.all_gather(outer_next.astype(jnp.bfloat16), "replica", axis=0, tiled=True)
+    my_tile = outer_next.astype(jnp.bfloat16)
+    synced = jnp.concatenate(
+        lax.all_to_all(
+            jnp.stack([my_tile for _ in range(lax.axis_size("replica"))]), "replica", 0, 0
+        ),
+        axis=0,
+    )
     return (outer_next[None], moment_next[None], synced[None])
 
 

time: 876 us -> 781 us (0.89)
  the two profiles are of different devices: /device:TPU:1 before, /device:TPU:33 now
where the time goes in v1:
time: 781 us; the launch traced here: 780 us
  waiting for transfers between devices  732 us (94%)
  starting transfers between devices  17.3 us (2%)
  between operations  15.6 us (2%)
    reduce_scatter x1, waiting for transfers between devices, owned_sum(): lax.psum_scatter(local_params.astype(jnp.float32), 'replica', scatter_dim...  673 us
    all_to_all x1, waiting for transfers between devices, sync_fragment(): lax.all_to_all(jnp.stack([my_tile for _ in range(lax.axis_size('replica')...  58.8 us
    all_to_all x1, starting transfers between devices, sync_fragment(): lax.all_to_all(jnp.stack([my_tile for _ in range(lax.axis_size('replica')...  17.2 us
  transfers between devices with their start and end apart: 3, of which 2 were waited for; matrix products, arithmetic and copies ran while one was open for 1% of the time, Pallas kernels for 0%

profile of v1, /device:TPU:33, one launch (start us, length us, event | category | flops | bytes accessed | tf_op | source)
XLA Modules:
  0.0 780.3 jit_solution(4626228207602336604)
XLA Ops:
  8.0 0.0 copy-start
  8.0 0.0 copy-start.4
  8.0 0.0 copy-start.1
  8.0 0.0 reduce-scatter.2.cloned.1.call-start
  8.1 3.0 bitcast_convert_fusion
  11.1 0.0 reduce-scatter.2.cloned.1.call-update
  11.1 0.0 all-gather.2.cloned.1.call-start
  11.2 0.0 copy-done.4
  11.2 0.0 copy-done.1
  11.2 0.0 copy-start.2
  11.2 0.0 copy-start.3
  11.2 0.3 fusion
  11.6 1.3 fusion.2
  12.8 0.0 all-gather.2.cloned.1.call-update
  12.9 672.8 %reduce-scatter.2.cloned.1.call-done = f32[16,512]{1,0:T(8,128)} async-done(((f32[1024,512]{1,0:T(8,128)}), f32[16,512]{1,0:T(8,128)}) %reduce-scatter.2.cloned.1.call-update) | async-done | bytes 32784 | tf_op jit(solution)/shard_map/reduce_scatter | solution.py:51
  685.6 0.0 copy-done.2
  685.6 1.4 fusion.17
  687.0 1.2 stack.2
  688.2 17.2 %all-to-all-start = ((bf16[64,16,512]{2,1,0:T(8,128)(2,1)}), bf16[64,16,512]{2,1,0:T(8,128)(2,1)S(1)}, u32[]{:S(2)}, u32[]{:S(2)}) async-start(bf16[64,16,512]{2,1,0:T(8,128)(2,1)} %stack.2), calls=%async_computation.1 | async-start | bytes 2097152 | tf_op jit(solution)/shard_map/all_to_all | solution.py:63
  705.5 58.8 %all-to-all-done = bf16[64,16,512]{2,1,0:T(8,128)(2,1)S(1)} async-done(((bf16[64,16,512]{2,1,0:T(8,128)(2,1)}), bf16[64,16,512]{2,1,0:T(8,128)(2,1)S(1)}, u32[]{:S(2)}, u32[]{:S(2)}) %all-to-all-start) | async-done | bytes 1048608 | tf_op jit(solution)/shard_map/all_to_all | solution.py:63
  764.2 6.3 fusion.5
  770.5 0.6 fusion.13
  771.1 0.8 copy.10
  771.9 1.0 copy.12
  (8 shorter events, 0.0 us)
Async XLA Ops:
  8.0 756.2 %copy-start = (bf16[1,8192,128]{2,1,0:T(8,128)(2,1)S(1)}, bf16[1,8192,128]{2,1,0:T(8,128)(2,1)}, u32[]{:S(2)}) copy-start(bf16[1,8192,128]{2,1,0:T(8,128)(2,1)} %param.8) | copy-start | bytes 6291460
  8.0 3.2 copy-start.4
  8.0 3.2 copy-start.1
  8.0 677.6 %reduce-scatter.2.cloned.1.call-start = ((), (), s32[]{:S(2)}) async-start(), calls=%async_computation.3 | async-start | bytes 2129920 | tf_op jit(solution)/shard_map/reduce_scatter | solution.py:51
  11.1 753.1 %all-gather.2.cloned.1.call-start = ((), (), s32[]{:S(2)}) async-start(), calls=%async_computation.2 | async-start | bytes 9437184 | tf_op jit(solution)/shard_map/all_gather | solution.py:37
  11.2 674.4 %copy-start.2 = (f32[1,16,512]{2,1,0:T(8,128)S(1)}, f32[1,16,512]{2,1,0:T(8,128)}, u32[]{:S(2)}) copy-start(f32[1,16,512]{2,1,0:T(8,128)} %param.11) | copy-start | bytes 98308
  11.2 674.4 %copy-start.3 = (f32[1,16,512]{2,1,0:T(8,128)S(1)}, f32[1,16,512]{2,1,0:T(8,128)}, u32[]{:S(2)}) copy-start(f32[1,16,512]{2,1,0:T(8,128)} %param.10) | copy-start | bytes 98308
  688.2 76.0 %all-to-all-start = ((bf16[64,16,512]{2,1,0:T(8,128)(2,1)}), bf16[64,16,512]{2,1,0:T(8,128)(2,1)S(1)}, u32[]{:S(2)}, u32[]{:S(2)}) async-start(bf16[64,16,512]{2,1,0:T(8,128)(2,1)} %stack.2), calls=%async_computation.1 | async-start | bytes 2097152 | tf_op jit(solution)/shard_map/all_to_all | solution.py:63
Sparse Core Ops, SparseCore 0:
  11.7 673.9 reduce-scatter.1
Sparse Core Ops, SparseCore 1:
  14.3 180.6 all-gather.1
